TPU v7x, 128 devices: a whole 4x4x4 slice. The times are simulated.
128 devices in a mesh: dp: 4 (over y), dict: 32 (over x, z, core).
Axes of the slice: x: 4, y: 4, z: 4, core: 2. Of those that a mesh axis runs over, the one named last changes fastest.
Arguments:
- acts: bfloat16 [8192, 8192], P('dict', 'dp'), may hold values from -6 to 6
- lists: int32 [512, 2], P('dict'), may hold values from 0 to 31, all different within a row; in each aligned block of 16 rows (0 to 15, 16 to 31, ...) at most 2 rows name the same one
- w_enc: bfloat16 [8192, 32768], P('dp', 'dict'), may hold values from -0.0625 to 0.0625
- w_dec: bfloat16 [32768, 8192], P('dict', 'dp'), may hold values from -0.1875 to 0.1875
- b_enc: bfloat16 [32768], P('dict'), may hold values from -3 to 3
- b_dec: bfloat16 [8192], P('dp'), may hold values from -3 to 3
Outputs:
- grad_enc: bfloat16 [8192, 32768], P('dp', 'dict')
- grad_dec: bfloat16 [32768, 8192], P('dict', 'dp')
Inputs may be any that keep to these rules, and one draw needn't show every extreme that they name: Each row block lists 2 different panels. Among the 16 row blocks of one index of dict, no panel is listed by more than 2 blocks, and some panel is listed by exactly 2.
All inputs are finite; a program needn't handle non-finite values.
Results may differ from a plain program's by a relative error of at most 0.0057.
Values may be sent and summed in bfloat16 or wider, within the bound.
No kernel may reach another device: no remote copies, remote signals or barrier semaphores. Data moves between devices by JAX's collectives and lax.ppermute only.
A program may use at most 128 MiB of HBM per device.

v0:
```python
import jax
import jax.numpy as jnp
from jax import lax
from jax.sharding import PartitionSpec as P


def on_device(acts, lists, w_enc, w_dec, b_enc, b_dec):
    peers = lax.axis_size("dict")
    block_count = lists.shape[0]
    active_count = lists.shape[1]
    rows_block = acts.shape[0] // block_count
    feature_cols = acts.shape[1]
    capacity = max(2, (2 * block_count * active_count + peers - 1) // peers)
    slot_total = peers * capacity
    flat_ids = lists.reshape(-1)
    onehot = (flat_ids[:, None] == jnp.arange(peers, dtype=jnp.int32)[None, :]).astype(jnp.int32)
    rank_index = jnp.sum((jnp.cumsum(onehot, axis=0) - 1) * onehot, axis=1)
    slot_index = flat_ids * capacity + rank_index
    item_block = jnp.arange(block_count * active_count, dtype=jnp.int32) // active_count
    slot_match = (jnp.arange(slot_total, dtype=jnp.int32)[:, None] == slot_index[None, :]).astype(
        jnp.float32
    )
    block_match = (item_block[:, None] == jnp.arange(block_count, dtype=jnp.int32)[None, :]).astype(
        jnp.float32
    )
    selector = jnp.dot(slot_match, block_match).astype(jnp.bfloat16)
    block_rows = acts.reshape(block_count, rows_block * feature_cols)
    outgoing = jnp.dot(selector, block_rows, preferred_element_type=jnp.float32).astype(
        jnp.bfloat16
    )
    outgoing = outgoing.reshape(peers, capacity * rows_block, feature_cols)
    received = lax.all_to_all(outgoing, "dict", split_axis=0, concat_axis=0, tiled=True)
    rows_in = received.reshape(-1, feature_cols)
    pre_local = jnp.dot(rows_in, w_enc, preferred_element_type=jnp.float32)
    bias_enc = b_enc.astype(jnp.float32)
    preact = lax.psum(pre_local, "dp") + bias_enc
    activity = (jnp.maximum(preact, 0.0) ** 2).astype(jnp.bfloat16)
    part = jnp.dot(activity, w_dec, preferred_element_type=jnp.float32).astype(jnp.bfloat16)
    part = part.reshape(peers, capacity * rows_block, feature_cols)
    returned = lax.all_to_all(part, "dict", split_axis=0, concat_axis=0, tiled=True)
    returned = returned.reshape(slot_total, rows_block * feature_cols)
    rebuilt = lax.dot_general(
        selector, returned, (((0,), (0,)), ((), ())), preferred_element_type=jnp.float32
    )
    rebuilt = rebuilt.reshape(block_count * rows_block, feature_cols) + b_dec.astype(jnp.float32)
    residual_g = ((rebuilt - acts.astype(jnp.float32)) * (1.0 / rows_block)).astype(jnp.bfloat16)
    resid_out = jnp.dot(
        selector,
        residual_g.reshape(block_count, rows_block * feature_cols),
        preferred_element_type=jnp.float32,
    ).astype(jnp.bfloat16)
    resid_out = resid_out.reshape(peers, capacity * rows_block, feature_cols)
    residual_in = lax.all_to_all(
        resid_out, "dict", split_axis=0, concat_axis=0, tiled=True
    ).reshape(-1, feature_cols)
    grad_dec = lax.dot_general(
        activity, residual_in, (((0,), (0,)), ((), ())), preferred_element_type=jnp.float32
    ).astype(jnp.bfloat16)
    dact_local = lax.dot_general(
        residual_in, w_dec, (((1,), (1,)), ((), ())), preferred_element_type=jnp.float32
    )
    dact = lax.psum(dact_local, "dp")
    grad_pre = (dact * 2.0 * jnp.maximum(preact, 0.0)).astype(jnp.bfloat16)
    grad_enc = lax.dot_general(
        rows_in, grad_pre, (((0,), (0,)), ((), ())), preferred_element_type=jnp.float32
    ).astype(jnp.bfloat16)
    return (grad_enc, grad_dec)


def solution(mesh):
    in_specs = (
        P("dict", "dp"),
        P("dict", None),
        P("dp", "dict"),
        P("dict", "dp"),
        P("dict"),
        P("dp"),
    )
    out_specs = (P("dp", "dict"), P("dict", "dp"))
    return jax.shard_map(
        on_device, mesh=mesh, in_specs=in_specs, out_specs=out_specs, check_vma=False
    )
```

profile of v0, /device:TPU:1, one launch (start us, length us, event | category | flops | bytes accessed | tf_op | source)
XLA Modules:
  0.0 449.6 jit_solution(6548300190928002087)
XLA Ops:
  7.2 0.0 all-reduce.3.cloned.1.call-start
  7.2 0.8 copy.9
  8.0 0.1 reshape.58
  8.1 0.1 fusion.4
  8.1 0.1 reduce_window_sum.11
  8.2 0.2 select_reduce_fusion
  8.4 1.6 reshape.59
  9.9 0.2 convolution_convert_fusion.5
  10.2 3.3 convolution_convert_fusion.1
  13.5 7.4 %reshape.60 = bf16[32,32,2048]{2,1,0:T(8,128)(2,1)} reshape(bf16[64,32768]{1,0:T(8,128)(2,1)} %convolution_convert_fusion.1) | data formatting | bytes 8388608 | tf_op jit(solution)/shard_map/reshape | solution.py:31
  20.9 0.0 copy-start.5
  20.9 60.3 %all_to_all.15 = bf16[32,32,2048]{2,1,0:T(8,128)(2,1)S(1)} all-to-all(bf16[32,32,2048]{2,1,0:T(8,128)(2,1)} %reshape.60), channel_id=1, replica_groups=mesh['dp'=4,'dict'=32] {'dict'}, dimensions={0} | all-to-all | bytes 8388608 | tf_op jit(solution)/shard_map/all_to_all | solution.py:32
  81.2 0.0 copy-start
  81.2 2.0 copy-done
  83.1 0.0 copy-done.5
  83.1 6.0 %fusion.10 = f32[1024,1024]{1,0:T(8,128)} fusion(bf16[1024,2048]{1,0:T(8,128)(2,1)S(1)} %bitcast.16, bf16[2048,1024]{1,0:T(8,128)(2,1)S(1)} %copy-done.5), kind=kOutput, calls=%fused_computation.29 | convolution fusion | flops 4294967296 | bytes 12582912 | tf_op jit(solution)/shard_map/dot_general | solution.py:34
  89.1 0.0 copy-start.4
  89.1 0.0 all-reduce.3.cloned.1.call-update
  89.1 0.7 copy-done.4
  89.8 89.8 %all-reduce.3.cloned.1.call-done = f32[1024,1024]{1,0:T(8,128)} async-done(((f32[1024,1024]{1,0:T(8,128)}), f32[1024,1024]{1,0:T(8,128)}) %all-reduce.3.cloned.1.call-update) | async-done | bytes 4194320 | tf_op jit(solution)/shard_map/psum | solution.py:36
  179.6 10.0 %convolution_convert_fusion.4 = bf16[1024,2048]{1,0:T(8,128)(2,1)} fusion(bf16[1024,2048]{1,0:T(8,128)(2,1)} %param.9, f32[1024,1024]{1,0:T(8,128)} %all-reduce.3.cloned.1.call-done, f32[1024]{0:T(1024)S(1)} %convert_element_type.44), kind=kOutput, calls=%fused_computation.7 | convolution fusion | flops 4301258752 | bytes 12587008 | tf_op jit(solution)/shard_map/dot_general | solution.py:38
  189.6 0.0 copy-start.3
  189.6 8.0 %all-to-all-start.1 = ((bf16[32,32,2048]{2,1,0:T(8,128)(2,1)}), bf16[32,32,2048]{2,1,0:T(8,128)(2,1)}, u32[]{:S(2)}, u32[]{:S(2)}) async-start(bf16[32,32,2048]{2,1,0:T(8,128)(2,1)} %bitcast.20), calls=%async_computation.1 | async-start | bytes 8388608 | tf_op jit(solution)/shard_map/all_to_all | solution.py:40
  197.6 0.0 all-reduce.5.cloned.1.call-start
  197.7 0.0 copy-done.3
  197.7 52.0 %all-to-all-done.1 = bf16[32,32,2048]{2,1,0:T(8,128)(2,1)} async-done(((bf16[32,32,2048]{2,1,0:T(8,128)(2,1)}), bf16[32,32,2048]{2,1,0:T(8,128)(2,1)}, u32[]{:S(2)}, u32[]{:S(2)}) %all-to-all-start.1) | async-done | bytes 4194336 | tf_op jit(solution)/shard_map/all_to_all | solution.py:40
  249.7 7.4 %reshape.63 = bf16[64,32768]{1,0:T(8,128)(2,1)} reshape(bf16[32,32,2048]{2,1,0:T(8,128)(2,1)} %all-to-all-done.1) | data formatting | bytes 8388608 | tf_op jit(solution)/shard_map/reshape | solution.py:41
  257.1 0.0 copy-start.2
  257.1 4.3 fusion.11
  261.4 1.7 reshape.64
  263.1 0.0 copy-done.2
  263.1 1.3 multiply_convert_fusion.3
  264.5 1.6 reshape.65
  266.0 3.3 convolution_convert_fusion
  269.3 7.4 %reshape.66 = bf16[32,32,2048]{2,1,0:T(8,128)(2,1)} reshape(bf16[64,32768]{1,0:T(8,128)(2,1)} %convolution_convert_fusion) | data formatting | bytes 8388608 | tf_op jit(solution)/shard_map/reshape | solution.py:52
  276.7 0.0 copy-start.6
  276.7 57.9 %all_to_all.16 = bf16[32,32,2048]{2,1,0:T(8,128)(2,1)S(1)} all-to-all(bf16[32,32,2048]{2,1,0:T(8,128)(2,1)} %reshape.66), channel_id=1, replica_groups=mesh['dp'=4,'dict'=32] {'dict'}, dimensions={0} | all-to-all | bytes 8388608 | tf_op jit(solution)/shard_map/all_to_all | solution.py:53
  334.6 0.0 copy-start.1
  334.6 1.9 copy-done.1
  336.5 0.0 copy-done.6
  336.5 6.1 %fusion.12 = f32[1024,1024]{1,0:T(8,128)} fusion(bf16[1024,2048]{1,0:T(8,128)(2,1)S(1)} %bitcast.18, bf16[1024,2048]{1,0:T(8,128)(2,1)S(1)} %copy-done.6), kind=kOutput, calls=%fused_computation.31 | convolution fusion | flops 4294967296 | bytes 12582912 | tf_op jit(solution)/shard_map/dot_general | solution.py:59
  342.6 0.0 all-reduce.5.cloned.1.call-update
  342.6 10.1 %convolution_convert_fusion.2 = bf16[1024,2048]{1,0:T(8,128)(2,1)} fusion(bf16[1024,2048]{1,0:T(8,128)(2,1)} %bitcast.19, f32[1024,1024]{1,0:T(8,128)} %all-reduce.3.cloned.1.call-done, f32[1024]{0:T(1024)S(1)} %convert_element_type.44), kind=kOutput, calls=%fused_computation.5 | convolution fusion | flops 4301258752 | bytes 12587008 | tf_op jit(solution)/shard_map/dot_general | solution.py:56
  352.7 78.8 %all-reduce.5.cloned.1.call-done = f32[1024,1024]{1,0:T(8,128)} async-done(((f32[1024,1024]{1,0:T(8,128)}), f32[1024,1024]{1,0:T(8,128)}) %all-reduce.5.cloned.1.call-update) | async-done | bytes 4194320 | tf_op jit(solution)/shard_map/psum | solution.py:62
  431.5 11.3 %convolution_convert_fusion.3 = bf16[2048,1024]{1,0:T(8,128)(2,1)} fusion(bf16[1024,2048]{1,0:T(8,128)(2,1)} %bitcast.17, f32[1024,1024]{1,0:T(8,128)} %all-reduce.5.cloned.1.call-done, f32[1024,1024]{1,0:T(8,128)} %all-reduce.3.cloned.1.call-done, f32[1024]{0:T(1024)S(1)} %convert_element_type.44), kind=kOutput, calls=%fused_computation.6 | convolution fusion | flops 4302307328 | bytes 16781312 | tf_op jit(solution)/shard_map/dot_general | solution.py:64
  (3 shorter events, 0.0 us)
Async XLA Ops:
  7.2 172.5 %all-reduce.3.cloned.1.call-start = ((), (), s32[]{:S(2)}) async-start(), calls=%async_computation.3 | async-start | bytes 8388608 | tf_op jit(solution)/shard_map/psum | solution.py:36
  20.9 62.3 %copy-start.5 = (bf16[2048,1024]{1,0:T(8,128)(2,1)S(1)}, bf16[2048,1024]{1,0:T(8,128)(2,1)}, u32[]{:S(2)}) copy-start(bf16[2048,1024]{1,0:T(8,128)(2,1)} %param.8) | copy-start | bytes 12582916
  81.2 2.0 copy-start
  89.1 0.7 copy-start.4
  189.6 8.1 %copy-start.3 = (bf16[2048]{0:T(1024)(128)(2,1)S(1)}, bf16[2048]{0:T(1024)(128)(2,1)}, u32[]{:S(2)}) copy-start(bf16[2048]{0:T(1024)(128)(2,1)} %param.11) | copy-start | bytes 12292
  189.6 60.1 %all-to-all-start.1 = ((bf16[32,32,2048]{2,1,0:T(8,128)(2,1)}), bf16[32,32,2048]{2,1,0:T(8,128)(2,1)}, u32[]{:S(2)}, u32[]{:S(2)}) async-start(bf16[32,32,2048]{2,1,0:T(8,128)(2,1)} %bitcast.20), calls=%async_computation.1 | async-start | bytes 8388608 | tf_op jit(solution)/shard_map/all_to_all | solution.py:40
  197.6 233.8 %all-reduce.5.cloned.1.call-start = ((), (), s32[]{:S(2)}) async-start(), calls=%async_computation.4 | async-start | bytes 8388608 | tf_op jit(solution)/shard_map/psum | solution.py:62
  257.1 6.0 %copy-start.2 = (bf16[256,2048]{1,0:T(8,128)(2,1)S(1)}, bf16[256,2048]{1,0:T(8,128)(2,1)}, u32[]{:S(2)}) copy-start(bf16[256,2048]{1,0:T(8,128)(2,1)} %param.6) | copy-start | bytes 3145732
  276.7 59.9 %copy-start.6 = (bf16[1024,2048]{1,0:T(8,128)(2,1)S(1)}, bf16[1024,2048]{1,0:T(8,128)(2,1)}, u32[]{:S(2)}) copy-start(bf16[1024,2048]{1,0:T(8,128)(2,1)} %param.9) | copy-start | bytes 12582916
  334.6 1.9 copy-start.1
Sparse Core Ops, SparseCore 0:
  89.3 90.3 all-reduce.2
  342.7 88.6 all-reduce.4
where the time goes:
time: 450 us
  waiting for transfers between devices  221 us (49%)
  blocking collectives  118 us (26%)
  matrix products  54.5 us (12%)
  local copies, waits for them, and re-layouts  32.4 us (7%)
  between operations  14.1 us (3%)
  starting transfers between devices  8.1 us (2%)
    psum x1, waiting for transfers between devices, on_device(): preact = lax.psum(pre_local, 'dp') + bias_enc  89.8 us
    psum x1, waiting for transfers between devices, on_device(): dact = lax.psum(dact_local, 'dp')  78.8 us
    all_to_all x1, blocking collectives, on_device(): lax.all_to_all(outgoing, 'dict', split_axis=0, concat_axis=0, tiled=True)  60.3 us
    all_to_all x1, blocking collectives, on_device(): lax.all_to_all(resid_out, 'dict', split_axis=0, concat_axis=0, tiled=True)  57.9 us
    all_to_all x1, waiting for transfers between devices, on_device(): lax.all_to_all(part, 'dict', split_axis=0, concat_axis=0, tiled=True)  52 us
    dot_general x1, matrix products, on_device(): lax.dot_general(rows_in, grad_pre, (((0,), (0,)), ((), ())), preferred_el...  11.3 us
    dot_general x1, matrix products, on_device(): lax.dot_general(activity, residual_in, (((0,), (0,)), ((), ())), preferre...  10.1 us
    dot_general x1, matrix products, on_device(): jnp.dot(activity, w_dec, preferred_element_type=jnp.float32)  9.98 us
  transfers between devices with their start and end apart: 3, of which 3 were waited for; matrix products, arithmetic and copies ran while one was open for 2% of the time, Pallas kernels for 0%

commit v1 on v0

--- a/solution.py
+++ b/solution.py
@@ -59,7 +59,10 @@
     dact_local = lax.dot_general(
         residual_in, w_dec, (((1,), (1,)), ((), ())), preferred_element_type=jnp.float32
     )
-    dact = lax.psum(dact_local, "dp")
+    size, dact = (lax.axis_size("dp"), dact_local)
+    for far in [1 << k for k in range(size.bit_length() - 1)]:
+        swap = [(i, i ^ far) for i in range(size)]
+        dact = dact + lax.ppermute(dact, "dp", swap)
     grad_pre = (dact * 2.0 * jnp.maximum(preact, 0.0)).astype(jnp.bfloat16)
     grad_enc = lax.dot_general(
         rows_in, grad_pre, (((0,), (0,)), ((), ())), preferred_element_type=jnp.float32

time: 450 us -> 540 us (1.20)
  waiting for transfers between devices: 221 us -> 319 us
  matrix products: 54.5 us -> 44.3 us
    ppermute x0 -> x2, waiting for transfers between devices: none -> 177 us  [on_device(): dact = dact + lax.ppermute(dact, 'dp', swap)]
    psum x1 -> x0, waiting for transfers between devices: 78.8 us -> none  [on_device(): dact = lax.psum(dact_local, 'dp')]
  transfers between devices with their start and end apart: 3 -> 4, of which waited for: 3 -> 4; matrix products, arithmetic and copies ran while one was open for 2% -> 1% of each run, Pallas kernels for 0% -> 0%
where the time goes in v1:
time: 540 us; the launch traced here: 538 us
  waiting for transfers between devices  319 us (59%)
  blocking collectives  118 us (22%)
  matrix products  44.3 us (8%)
  local copies, waits for them, and re-layouts  30.5 us (6%)
  between operations  14.1 us (3%)
  starting transfers between devices  9.61 us (2%)
    ppermute x2, waiting for transfers between devices, on_device(): dact = dact + lax.ppermute(dact, 'dp', swap)  177 us
    psum x1, waiting for transfers between devices, on_device(): preact = lax.psum(pre_local, 'dp') + bias_enc  89.8 us
    all_to_all x1, blocking collectives, on_device(): lax.all_to_all(outgoing, 'dict', split_axis=0, concat_axis=0, tiled=True)  60.3 us
    all_to_all x1, blocking collectives, on_device(): lax.all_to_all(resid_out, 'dict', split_axis=0, concat_axis=0, tiled=True)  57.9 us
    all_to_all x1, waiting for transfers between devices, on_device(): lax.all_to_all(part, 'dict', split_axis=0, concat_axis=0, tiled=True)  52.1 us
  transfers between devices with their start and end apart: 4, of which 4 were waited for; matrix products, arithmetic and copies ran while one was open for 1% of the time, Pallas kernels for 0%

profile of v1, /device:TPU:1, one launch (start us, length us, event | category | flops | bytes accessed | tf_op | source)
XLA Modules:
  0.0 538.3 jit_solution(11361581139872615480)
XLA Ops:
  7.2 0.0 all-reduce.2.cloned.1.call-start
  7.2 0.8 copy.9
  8.0 0.1 reshape.58
  8.1 0.1 fusion.4
  8.1 0.1 reduce_window_sum.11
  8.2 0.2 select_reduce_fusion
  8.4 1.6 reshape.59
  9.9 0.2 convolution_convert_fusion.5
  10.2 3.3 convolution_convert_fusion.1
  13.5 7.4 %reshape.60 = bf16[32,32,2048]{2,1,0:T(8,128)(2,1)} reshape(bf16[64,32768]{1,0:T(8,128)(2,1)} %convolution_convert_fusion.1) | data formatting | bytes 8388608 | tf_op jit(solution)/shard_map/reshape | solution.py:31
  20.9 0.0 copy-start.5
  20.9 60.3 %all_to_all.15 = bf16[32,32,2048]{2,1,0:T(8,128)(2,1)S(1)} all-to-all(bf16[32,32,2048]{2,1,0:T(8,128)(2,1)} %reshape.60), channel_id=1, replica_groups=mesh['dp'=4,'dict'=32] {'dict'}, dimensions={0} | all-to-all | bytes 8388608 | tf_op jit(solution)/shard_map/all_to_all | solution.py:32
  81.2 0.0 copy-start
  81.2 2.0 copy-done
  83.2 0.0 copy-done.5
  83.2 6.0 %fusion.10 = f32[1024,1024]{1,0:T(8,128)} fusion(bf16[1024,2048]{1,0:T(8,128)(2,1)S(1)} %bitcast.16, bf16[2048,1024]{1,0:T(8,128)(2,1)S(1)} %copy-done.5), kind=kOutput, calls=%fused_computation.29 | convolution fusion | flops 4294967296 | bytes 12582912 | tf_op jit(solution)/shard_map/dot_general | solution.py:34
  89.2 0.0 copy-start.4
  89.2 0.0 all-reduce.2.cloned.1.call-update
  89.2 0.7 copy-done.4
  89.8 89.8 %all-reduce.2.cloned.1.call-done = f32[1024,1024]{1,0:T(8,128)} async-done(((f32[1024,1024]{1,0:T(8,128)}), f32[1024,1024]{1,0:T(8,128)}) %all-reduce.2.cloned.1.call-update) | async-done | bytes 4194320 | tf_op jit(solution)/shard_map/psum | solution.py:36
  179.7 10.0 %convolution_convert_fusion.4 = bf16[1024,2048]{1,0:T(8,128)(2,1)} fusion(bf16[1024,2048]{1,0:T(8,128)(2,1)} %param.9, f32[1024,1024]{1,0:T(8,128)} %all-reduce.2.cloned.1.call-done, f32[1024]{0:T(1024)S(1)} %convert_element_type.44), kind=kOutput, calls=%fused_computation.7 | convolution fusion | flops 4301258752 | bytes 12587008 | tf_op jit(solution)/shard_map/dot_general | solution.py:38
  189.6 0.0 copy-start.3
  189.6 8.0 %all-to-all-start.1 = ((bf16[32,32,2048]{2,1,0:T(8,128)(2,1)}), bf16[32,32,2048]{2,1,0:T(8,128)(2,1)}, u32[]{:S(2)}, u32[]{:S(2)}) async-start(bf16[32,32,2048]{2,1,0:T(8,128)(2,1)} %bitcast.20), calls=%async_computation.1 | async-start | bytes 8388608 | tf_op jit(solution)/shard_map/all_to_all | solution.py:40
  197.7 0.0 copy-done.3
  197.7 52.1 %all-to-all-done.1 = bf16[32,32,2048]{2,1,0:T(8,128)(2,1)} async-done(((bf16[32,32,2048]{2,1,0:T(8,128)(2,1)}), bf16[32,32,2048]{2,1,0:T(8,128)(2,1)}, u32[]{:S(2)}, u32[]{:S(2)}) %all-to-all-start.1) | async-done | bytes 4194336 | tf_op jit(solution)/shard_map/all_to_all | solution.py:40
  249.8 7.4 %reshape.63 = bf16[64,32768]{1,0:T(8,128)(2,1)} reshape(bf16[32,32,2048]{2,1,0:T(8,128)(2,1)} %all-to-all-done.1) | data formatting | bytes 8388608 | tf_op jit(solution)/shard_map/reshape | solution.py:41
  257.2 0.0 copy-start.2
  257.2 4.3 fusion.11
  261.4 1.7 reshape.64
  263.2 0.0 copy-done.2
  263.2 1.3 multiply_convert_fusion.3
  264.5 1.6 reshape.65
  266.1 3.3 convolution_convert_fusion
  269.4 7.4 %reshape.66 = bf16[32,32,2048]{2,1,0:T(8,128)(2,1)} reshape(bf16[64,32768]{1,0:T(8,128)(2,1)} %convolution_convert_fusion) | data formatting | bytes 8388608 | tf_op jit(solution)/shard_map/reshape | solution.py:52
  276.8 0.0 copy-start.6
  276.8 57.9 %all_to_all.16 = bf16[32,32,2048]{2,1,0:T(8,128)(2,1)S(1)} all-to-all(bf16[32,32,2048]{2,1,0:T(8,128)(2,1)} %reshape.66), channel_id=1, replica_groups=mesh['dp'=4,'dict'=32] {'dict'}, dimensions={0} | all-to-all | bytes 8388608 | tf_op jit(solution)/shard_map/all_to_all | solution.py:53
  334.7 0.0 copy-done.6
  334.7 4.5 fusion.12
  339.2 0.0 copy-start.7
  339.2 0.2 collective-permute-start
  339.4 91.9 %collective-permute-done = f32[1024,1024]{1,0:T(8,128)S(1)} collective-permute-done((f32[1024,1024]{1,0:T(8,128)S(1)}, f32[1024,1024]{1,0:T(8,128)S(1)}, u32[]{:S(2)}, u32[]{:S(2)}) %collective-permute-start) | collective-permute-done | bytes 4194336 | tf_op jit(solution)/shard_map/ppermute | solution.py:65
  431.3 1.0 add.42
  432.3 0.0 copy-start.1
  432.3 1.4 collective-permute-start.1
  433.7 0.0 copy-done.7
  433.7 6.3 %convolution_convert_fusion.2 = bf16[1024,2048]{1,0:T(8,128)(2,1)} fusion(bf16[1024,2048]{1,0:T(8,128)(2,1)S(1)} %bitcast.19, f32[1024,1024]{1,0:T(8,128)S(1)} %copy-done.7, f32[1024]{0:T(1024)S(1)} %convert_element_type.44), kind=kOutput, calls=%fused_computation.5 | convolution fusion | flops 4301258752 | bytes 12587008 | tf_op jit(solution)/shard_map/dot_general | solution.py:56
  440.0 85.1 %collective-permute-done.1 = f32[1024,1024]{1,0:T(8,128)S(1)} collective-permute-done((f32[1024,1024]{1,0:T(8,128)S(1)}, f32[1024,1024]{1,0:T(8,128)S(1)}, u32[]{:S(2)}, u32[]{:S(2)}) %collective-permute-start.1) | collective-permute-done | bytes 4194336 | tf_op jit(solution)/shard_map/ppermute | solution.py:65
  525.1 0.0 copy-done.1
  525.1 6.4 %convolution_convert_fusion.3 = bf16[2048,1024]{1,0:T(8,128)(2,1)} fusion(bf16[1024,2048]{1,0:T(8,128)(2,1)S(1)} %bitcast.17, f32[1024,1024]{1,0:T(8,128)S(1)} %add.42, f32[1024,1024]{1,0:T(8,128)S(1)} %collective-permute-done.1, f32[1024,1024]{1,0:T(8,128)S(1)} %copy-done.7, f32[1024]{0:T(1024)S(1)} %convert_element_type.44), kind=kOutput, calls=%fused_computation.6 | convolution fusion | flops 4303355904 | bytes 20975616 | tf_op jit(solution)/shard_map/dot_general | solution.py:67
  (3 shorter events, 0.0 us)
Async XLA Ops:
  7.2 172.5 %all-reduce.2.cloned.1.call-start = ((), (), s32[]{:S(2)}) async-start(), calls=%async_computation.3 | async-start | bytes 8388608 | tf_op jit(solution)/shard_map/psum | solution.py:36
  20.9 62.3 %copy-start.5 = (bf16[2048,1024]{1,0:T(8,128)(2,1)S(1)}, bf16[2048,1024]{1,0:T(8,128)(2,1)}, u32[]{:S(2)}) copy-start(bf16[2048,1024]{1,0:T(8,128)(2,1)} %param.8) | copy-start | bytes 12582916
  81.2 2.0 copy-start
  89.2 0.7 copy-start.4
  189.6 8.0 %copy-start.3 = (bf16[2048]{0:T(1024)(128)(2,1)S(1)}, bf16[2048]{0:T(1024)(128)(2,1)}, u32[]{:S(2)}) copy-start(bf16[2048]{0:T(1024)(128)(2,1)} %param.11) | copy-start | bytes 12292
  189.6 60.1 %all-to-all-start.1 = ((bf16[32,32,2048]{2,1,0:T(8,128)(2,1)}), bf16[32,32,2048]{2,1,0:T(8,128)(2,1)}, u32[]{:S(2)}, u32[]{:S(2)}) async-start(bf16[32,32,2048]{2,1,0:T(8,128)(2,1)} %bitcast.20), calls=%async_computation.1 | async-start | bytes 8388608 | tf_op jit(solution)/shard_map/all_to_all | solution.py:40
  257.2 6.0 %copy-start.2 = (bf16[256,2048]{1,0:T(8,128)(2,1)S(1)}, bf16[256,2048]{1,0:T(8,128)(2,1)}, u32[]{:S(2)}) copy-start(bf16[256,2048]{1,0:T(8,128)(2,1)} %param.6) | copy-start | bytes 3145732
  276.8 57.9 %copy-start.6 = (bf16[1024,2048]{1,0:T(8,128)(2,1)S(1)}, bf16[1024,2048]{1,0:T(8,128)(2,1)}, u32[]{:S(2)}) copy-start(bf16[1024,2048]{1,0:T(8,128)(2,1)} %param.9) | copy-start | bytes 12582916
  339.2 94.5 %copy-start.7 = (f32[1024,1024]{1,0:T(8,128)S(1)}, f32[1024,1024]{1,0:T(8,128)}, u32[]{:S(2)}) copy-start(f32[1024,1024]{1,0:T(8,128)} %all-reduce.2.cloned.1.call-done) | copy-start | bytes 12582916
  339.2 92.1 %collective-permute-start = (f32[1024,1024]{1,0:T(8,128)S(1)}, f32[1024,1024]{1,0:T(8,128)S(1)}, u32[]{:S(2)}, u32[]{:S(2)}) collective-permute-start(f32[1024,1024]{1,0:T(8,128)S(1)} %fusion.12), channel_id=1, source_target_pairs={{0,32},{32,0},{64,96},{96,64},{1,33},{33,1},{65,97},{97,65},{2,34}... | collective-permute-start | bytes 12582920 | tf_op jit(solution)/shard_map/ppermute | solution.py:65
  432.3 92.8 %copy-start.1 = (bf16[32,32,2048]{2,1,0:T(8,128)(2,1)S(1)}, bf16[32,32,2048]{2,1,0:T(8,128)(2,1)}, u32[]{:S(2)}) copy-start(bf16[32,32,2048]{2,1,0:T(8,128)(2,1)} %copy-done) | copy-start | bytes 12582916
  432.3 92.7 %collective-permute-start.1 = (f32[1024,1024]{1,0:T(8,128)S(1)}, f32[1024,1024]{1,0:T(8,128)S(1)}, u32[]{:S(2)}, u32[]{:S(2)}) collective-permute-start(f32[1024,1024]{1,0:T(8,128)S(1)} %add.42), channel_id=1, source_target_pairs={{0,64},{32,96},{64,0},{96,32},{1,65},{33,97},{65,1},{97,33},{2,66}... | collective-permute-start | bytes 12582920 | tf_op jit(solution)/shard_map/ppermute | solution.py:65
Sparse Core Ops, SparseCore 0:
  89.3 90.3 all-reduce.1
